TPU v7x, 128 devices: a whole 4x4x4 slice. The times are simulated.
128 devices in a mesh: expert: 16 (over z, x), group: 8 (over y, core).
Axes of the slice: x: 4, y: 4, z: 4, core: 2. Of those that a mesh axis runs over, the one named last changes fastest.
Arguments:
- activations: bfloat16 [16384, 2048], P(('expert', 'group')), may hold values from -24 to 24
- out_grad: bfloat16 [16384, 2048], P(('expert', 'group')), may hold values from -24 to 24
- combine_weights: bfloat16 [16384, 4], P(('expert', 'group')), may hold values from 0.099609375 to 0.5
- expert_ids: int32 [16384, 4], P(('expert', 'group')), may hold values from 0 to 15, all different within a row; in each aligned block of 128 rows (0 to 127, 128 to 255, ...) at most 96 rows name the same one
- gate_up_weight: bfloat16 [16, 2048, 1024], P('expert'), may hold values from -0.125 to 0.125
- down_weight: bfloat16 [16, 2048, 512], P('expert'), may hold values from -0.25 to 0.25
Outputs:
- grad_input: bfloat16 [16384, 2048], P(('expert', 'group'))
- grad_combine: bfloat16 [16384, 4], P(('expert', 'group'))
- grad_gate_up: float32 [16, 2048, 1024], P('expert', 'group')
- grad_down: float32 [16, 2048, 512], P('expert', 'group')
Inputs may be any that keep to these rules, and one draw needn't show every extreme that they name: `expert_ids`: each row names 4 different experts. Within the 128 rows of one device no expert is named more than 96 times, and in some device's rows an expert is named exactly 96 times.
All inputs are finite; a program needn't handle non-finite values.
Results may differ from a plain program's by a relative error of at most 0.0064.
Values may be sent and summed in bfloat16 or wider, within the bound.
A program may use at most 128 MiB of HBM per device.

v0:
```python
import jax
import jax.numpy as jnp
from jax import lax
from jax.sharding import PartitionSpec as P


def body(activations, out_grad, combine_weights, expert_ids, gate_up_weight, down_weight):
    experts_all = lax.axis_size("expert")
    me = lax.axis_index("expert")
    columns = jnp.arange(experts_all, dtype=jnp.int32)
    named = expert_ids[:, :, None] == columns[None, None, :]
    table = jnp.sum(
        jnp.where(named, combine_weights.astype(jnp.float32)[:, :, None], 0.0), axis=1
    ).astype(jnp.bfloat16)
    rows_x = lax.all_gather(activations, "expert", axis=0, tiled=True)
    rows_g = lax.all_gather(out_grad, "expert", axis=0, tiled=True)
    tables = lax.all_gather(table, "expert", axis=0, tiled=True)
    mine = (columns == me).astype(jnp.float32)
    rows_w = jnp.sum(tables.astype(jnp.float32) * mine[None, :], axis=1, keepdims=True)
    weight_gu = gate_up_weight[0]
    weight_down = down_weight[0]
    hidden_dim = weight_down.shape[1]
    pre = jnp.dot(rows_x, weight_gu, preferred_element_type=jnp.float32)
    gate = pre[:, :hidden_dim]
    upper = pre[:, hidden_dim:]
    sig = jax.nn.sigmoid(gate)
    hidden = (gate * sig * upper).astype(jnp.bfloat16).astype(jnp.float32)
    raw = jnp.dot(rows_g, weight_down, preferred_element_type=jnp.float32)
    prob = jnp.sum(hidden * raw, axis=1, keepdims=True)
    hidden_grad = raw * rows_w
    gate_grad = hidden_grad * upper * sig * (1.0 + gate * (1.0 - sig))
    upper_grad = hidden_grad * gate * sig
    pre_grad = jnp.concatenate([gate_grad, upper_grad], axis=1).astype(jnp.bfloat16)
    scaled = (hidden * rows_w).astype(jnp.bfloat16)
    slot_grad = lax.dot_general(
        pre_grad, weight_gu, (((1,), (1,)), ((), ())), preferred_element_type=jnp.float32
    ).astype(jnp.bfloat16)
    grad_input = lax.psum_scatter(slot_grad, "expert", scatter_dimension=0, tiled=True)
    probs = lax.psum_scatter(
        (prob * mine[None, :]).astype(jnp.bfloat16), "expert", scatter_dimension=0, tiled=True
    )
    grad_combine = jnp.sum(
        jnp.where(named, probs.astype(jnp.float32)[:, None, :], 0.0), axis=2
    ).astype(jnp.bfloat16)
    grad_gate_up = lax.psum_scatter(
        lax.dot_general(
            rows_x, pre_grad, (((0,), (0,)), ((), ())), preferred_element_type=jnp.float32
        ).astype(jnp.bfloat16),
        "group",
        scatter_dimension=0,
        tiled=True,
    ).astype(jnp.float32)
    grad_down = lax.psum_scatter(
        lax.dot_general(
            rows_g, scaled, (((0,), (0,)), ((), ())), preferred_element_type=jnp.float32
        ).astype(jnp.bfloat16),
        "group",
        scatter_dimension=0,
        tiled=True,
    ).astype(jnp.float32)
    return (grad_input, grad_combine, grad_gate_up[None], grad_down[None])


def solution(mesh):
    rows = P(("expert", "group"), None)
    return jax.shard_map(
        body,
        mesh=mesh,
        in_specs=(rows, rows, rows, rows, P("expert", None, None), P("expert", None, None)),
        out_specs=(rows, rows, P("expert", "group", None), P("expert", "group", None)),
        check_vma=False,
    )
```

profile of v0, /device:TPU:0, one launch (start us, length us, event | category | flops | bytes accessed | tf_op | source)
XLA Modules:
  0.0 444.1 jit_solution(17004456806041273709)
XLA Ops:
  7.2 0.0 copy-start
  7.2 0.0 all-gather.5.cloned.1.call-start
  7.2 0.7 all-gather.5.cloned.1.call-update
  7.9 0.0 all-gather.3.cloned.1.call-start
  8.0 0.7 all-gather.3.cloned.1.call-update
  8.7 0.0 reduce-scatter.13.cloned.1.call-start
  8.7 74.9 %all-gather.5.cloned.1.call-done = bf16[2048,2048]{1,0:T(8,128)(2,1)} async-done(((bf16[128,2048]{1,0:T(8,128)(2,1)}), bf16[2048,2048]{1,0:T(8,128)(2,1)}) %all-gather.5.cloned.1.call-update) | async-done | bytes 8388624 | tf_op jit(solution)/shard_map/all_gather | solution.py:15
  83.6 14.7 %fusion.3 = f32[2048,1024]{0,1:T(8,128)} fusion(bf16[2048,2048]{1,0:T(8,128)(2,1)} %all-gather.5.cloned.1.call-done, bf16[1,2048,1024]{2,1,0:T(8,128)(2,1)} %param.10), kind=kOutput, calls=%fused_computation.7 | convolution fusion | flops 8589934592 | bytes 20971520 | tf_op jit(solution)/shard_map/dot_general | solution.py:23
  98.2 0.0 copy-start.4
  98.2 0.0 copy-start.3
  98.2 58.0 %all-gather.3.cloned.1.call-done = bf16[2048,2048]{1,0:T(8,128)(2,1)} async-done(((bf16[128,2048]{1,0:T(8,128)(2,1)}), bf16[2048,2048]{1,0:T(8,128)(2,1)}) %all-gather.3.cloned.1.call-update) | async-done | bytes 8388624 | tf_op jit(solution)/shard_map/all_gather | solution.py:16
  156.3 0.0 copy-done
  156.3 11.9 %fusion = (f32[2048]{0:T(1024)S(1)}, bf16[2048,512]{0,1:T(8,128)(2,1)}, f32[2048,512]{0,1:T(8,128)}) fusion(f32[2048,1024]{0,1:T(8,128)} %fusion.3, bf16[2048,2048]{1,0:T(8,128)(2,1)} %all-gather.3.cloned.1.call-done, bf16[1,2048,512]{2,1,0:T(8,128)(2,1)S(1)} %copy-done), kind=kOutput, calls=%fused_computation.3 | convolution fusion | flops 4304402432 | bytes 25174016 | tf_op jit(solution)/shard_map/dot_general | solution.py:28
  168.2 0.1 multiply_convert_fusion.3
  168.2 1.0 copy.18
  169.2 0.0 reduce-scatter.13.cloned.1.call-update
  169.3 0.0 reduce-scatter.11.cloned.1.call-start
  169.3 0.0 copy-done.4
  169.3 73.2 %reduce-scatter.13.cloned.1.call-done = bf16[128,16]{1,0:T(8,128)(2,1)} async-done(((bf16[2048,16]{1,0:T(8,128)(2,1)}), bf16[128,16]{1,0:T(8,128)(2,1)}) %reduce-scatter.13.cloned.1.call-update) | async-done | bytes 4112
  242.6 0.8 copy.19
  243.4 0.0 copy-done.3
  243.4 0.6 select_reduce_fusion
  244.0 22.8 %all_gather.10 = bf16[2048,16]{0,1:T(8,128)(2,1)S(1)} all-gather(bf16[128,16]{0,1:T(8,128)(2,1)S(1)} %get-tuple-element.17), channel_id=1, replica_groups=mesh['expert'=16,'group'=8] {'expert'}, dimensions={0}, use_global_device_ids=true | all-gather | bytes 69632 | tf_op jit(solution)/shard_map/all_gather | solution.py:17
  266.8 0.1 multiply_reduce_fusion
  266.9 9.9 %fusion.5 = bf16[2048,512]{0,1:T(8,128)(2,1)} fusion(bf16[2048,2048]{1,0:T(8,128)(2,1)} %all-gather.3.cloned.1.call-done, bf16[2048,512]{0,1:T(8,128)(2,1)} %get-tuple-element.19, f32[2048]{0:T(1024)S(1)} %multiply_reduce_fusion), kind=kOutput, calls=%fused_computation.15 | convolution fusion | flops 4299161600 | bytes 12591104 | tf_op jit(solution)/shard_map/dot_general | solution.py:54
  276.8 0.0 reduce-scatter.11.cloned.1.call-update
  276.8 0.2 reduce-scatter.9.cloned.1.call-start
  277.0 5.7 %multiply_convert_fusion.2 = (bf16[2048,512]{0,1:T(8,128)(2,1)S(1)}, bf16[2048,512]{0,1:T(8,128)(2,1)S(1)}) fusion(f32[2048,1024]{0,1:T(8,128)} %fusion.3, f32[2048,512]{0,1:T(8,128)} %get-tuple-element.22, f32[2048]{0:T(1024)S(1)} %multiply_reduce_fusion), kind=kLoop, calls=%fused_computation.12 | loop fusion | flops 14680064 | bytes 16785408 | tf_op jit(solution)/shard_map/convert.2
  282.8 0.0 copy-start.1
  282.8 0.0 copy-start.2
  282.8 1.3 copy-done.1
  284.1 0.7 copy-done.2
  284.8 12.6 %convert_bitcast_fusion = bf16[2048,1024]{0,1:T(8,128)(2,1)} fusion(bf16[2048,2048]{1,0:T(8,128)(2,1)} %all-gather.5.cloned.1.call-done, bf16[2048,512]{0,1:T(8,128)(2,1)S(1)} %get-tuple-element.21, bf16[2048,512]{0,1:T(8,128)(2,1)S(1)} %get-tuple-element.20), kind=kOutput, calls=%fused_computation.9 | convolution fusion | flops 8600420352 | bytes 16777216 | tf_op jit(solution)/shard_map/dot_general | solution.py:46
  297.4 0.0 reduce-scatter.9.cloned.1.call-update
  297.5 0.0 reduce-scatter.7.cloned.1.call-start
  297.5 14.0 %convolution_convert_fusion = bf16[2048,2048]{1,0:T(8,128)(2,1)} fusion(bf16[1,2048,1024]{2,1,0:T(8,128)(2,1)} %param.10, bf16[2048,512]{0,1:T(8,128)(2,1)} %copy-done.2, bf16[2048,512]{0,1:T(8,128)(2,1)} %copy-done.1), kind=kOutput, calls=%fused_computation | convolution fusion | flops 8602517504 | bytes 16777216 | tf_op jit(solution)/shard_map/dot_general | solution.py:35
  311.5 0.0 reduce-scatter.7.cloned.1.call-update
  311.5 0.0 reduce-scatter.11.cloned.1.call-done
  311.6 1.0 bitcast_convert_fusion.1
  312.6 1.0 copy.17
  313.6 35.0 %reduce-scatter.9.cloned.1.call-done = bf16[256,1024]{0,1:T(8,128)(2,1)} async-done(((bf16[2048,1024]{0,1:T(8,128)(2,1)}), bf16[256,1024]{0,1:T(8,128)(2,1)}) %reduce-scatter.9.cloned.1.call-update) | async-done | bytes 524304 | tf_op jit(solution)/shard_map/reduce_scatter | solution.py:45
  348.5 1.1 bitcast_convert_fusion
  349.7 1.3 copy.16
  351.0 86.3 %reduce-scatter.7.cloned.1.call-done = bf16[128,2048]{1,0:T(8,128)(2,1)} async-done(((bf16[2048,2048]{1,0:T(8,128)(2,1)}), bf16[128,2048]{1,0:T(8,128)(2,1)}) %reduce-scatter.7.cloned.1.call-update) | async-done | bytes 524304 | tf_op jit(solution)/shard_map/reduce_scatter | solution.py:38
  (3 shorter events, 0.0 us)
Async XLA Ops:
  7.2 149.1 %copy-start = (bf16[1,2048,512]{2,1,0:T(8,128)(2,1)S(1)}, bf16[1,2048,512]{2,1,0:T(8,128)(2,1)}, u32[]{:S(2)}) copy-start(bf16[1,2048,512]{2,1,0:T(8,128)(2,1)} %param.11) | copy-start | bytes 6291460
  7.2 76.4 %all-gather.5.cloned.1.call-start = ((), (), s32[]{:S(2)}) async-start(), calls=%async_computation.5 | async-start | bytes 8912896 | tf_op jit(solution)/shard_map/all_gather | solution.py:15
  7.9 148.4 %all-gather.3.cloned.1.call-start = ((), (), s32[]{:S(2)}) async-start(), calls=%async_computation.4 | async-start | bytes 8912896 | tf_op jit(solution)/shard_map/all_gather | solution.py:16
  8.7 233.9 %reduce-scatter.13.cloned.1.call-start = ((), (), s32[]{:S(2)}) async-start(), calls=%async_computation.9 | async-start | bytes 557056
  98.2 71.1 %copy-start.4 = (bf16[128,4]{0,1:T(4,128)(2,1)S(1)}, bf16[128,4]{0,1:T(4,128)(2,1)}, u32[]{:S(2)}) copy-start(bf16[128,4]{0,1:T(4,128)(2,1)} %param.8) | copy-start | bytes 3076
  98.2 145.2 %copy-start.3 = (s32[128,4]{0,1:T(4,128)S(1)}, s32[128,4]{0,1:T(4,128)}, u32[]{:S(2)}) copy-start(s32[128,4]{0,1:T(4,128)} %param.9) | copy-start | bytes 6148
  169.3 142.3 %reduce-scatter.11.cloned.1.call-start = ((), (), s32[]{:S(2)}) async-start(), calls=%async_computation.8 | async-start | bytes 2359296 | tf_op jit(solution)/shard_map/reduce_scatter | solution.py:53
  276.8 71.7 %reduce-scatter.9.cloned.1.call-start = ((), (), s32[]{:S(2)}) async-start(), calls=%async_computation.7 | async-start | bytes 4718592 | tf_op jit(solution)/shard_map/reduce_scatter | solution.py:45
  282.8 1.3 copy-start.1
  282.8 2.0 copy-start.2
  297.5 139.8 %reduce-scatter.7.cloned.1.call-start = ((), (), s32[]{:S(2)}) async-start(), calls=%async_computation.6 | async-start | bytes 8912896 | tf_op jit(solution)/shard_map/reduce_scatter | solution.py:38
Sparse Core Ops, SparseCore 0:
  10.1 73.4 all-gather.4
  85.7 70.5 all-gather.2
  169.4 73.1 reduce-scatter.12
  276.9 32.4 reduce-scatter.10
  311.7 36.8 reduce-scatter.8
  352.4 84.8 reduce-scatter.6
where the time goes:
time: 444 us
  waiting for transfers between devices  329 us (74%)
  matrix products  63 us (14%)
  blocking collectives  22.8 us (5%)
  between operations  14.2 us (3%)
  other arithmetic  8.64 us (2%)
  local copies, waits for them, and re-layouts  6.14 us (1%)
    reduce_scatter x1, waiting for transfers between devices, body(): lax.psum_scatter(slot_grad, 'expert', scatter_dimension=0, tiled=True)  86.3 us
    all_gather x1, waiting for transfers between devices, body(): rows_x = lax.all_gather(activations, 'expert', axis=0, tiled=True)  74.9 us
    unnamed x7, waiting for transfers between devices  74.7 us
    all_gather x1, waiting for transfers between devices, body(): rows_g = lax.all_gather(out_grad, 'expert', axis=0, tiled=True)  58 us
    reduce_scatter x1, waiting for transfers between devices, body(): lax.psum_scatter(lax.dot_general(rows_x, pre_grad, (((0,), (0,)), ((), ()...  35 us
    all_gather x1, blocking collectives, body(): tables = lax.all_gather(table, 'expert', axis=0, tiled=True)  22.8 us
    dot_general x1, matrix products, body(): pre = jnp.dot(rows_x, weight_gu, preferred_element_type=jnp.float32)  14.7 us
    dot_general x1, matrix products, body(): lax.dot_general(pre_grad, weight_gu, (((1,), (1,)), ((), ())), preferred_...  14 us
  transfers between devices with their start and end apart: 6, of which 5 were waited for; matrix products, arithmetic and copies ran while one was open for 12% of the time, Pallas kernels for 0%

commit v1 on v0

--- a/solution.py
+++ b/solution.py
@@ -2,6 +2,24 @@
 import jax.numpy as jnp
 from jax import lax
 from jax.sharding import PartitionSpec as P
+
+
+def collect(array, axis, dim):
+    ways, here, step = (lax.axis_size(axis), lax.axis_index(axis), array.shape[dim])
+    shape = [n * ways if d == dim else n for d, n in enumerate(array.shape)]
+    full = lax.dynamic_update_slice_in_dim(
+        jnp.zeros(shape, array.dtype), array, here * step, axis=dim
+    )
+    going_up = going_down = array
+    for far in range(1, ways // 2 + 1):
+        going_up = lax.ppermute(going_up, axis, [(d, (d + 1) % ways) for d in range(ways)])
+        full = lax.dynamic_update_slice_in_dim(full, going_up, (here - far) % ways * step, axis=dim)
+        if 2 * far < ways:
+            going_down = lax.ppermute(going_down, axis, [(d, (d - 1) % ways) for d in range(ways)])
+            full = lax.dynamic_update_slice_in_dim(
+                full, going_down, (here + far) % ways * step, axis=dim
+            )
+    return full
 
 
 def body(activations, out_grad, combine_weights, expert_ids, gate_up_weight, down_weight):
@@ -13,7 +31,7 @@
         jnp.where(named, combine_weights.astype(jnp.float32)[:, :, None], 0.0), axis=1
     ).astype(jnp.bfloat16)
     rows_x = lax.all_gather(activations, "expert", axis=0, tiled=True)
-    rows_g = lax.all_gather(out_grad, "expert", axis=0, tiled=True)
+    rows_g = collect(out_grad, "expert", 0)
     tables = lax.all_gather(table, "expert", axis=0, tiled=True)
     mine = (columns == me).astype(jnp.float32)
     rows_w = jnp.sum(tables.astype(jnp.float32) * mine[None, :], axis=1, keepdims=True)

time: 444 us -> 464 us (1.045)
  waiting for transfers between devices: 329 us -> 286 us
  starting transfers between devices: 0.42 us -> 40.8 us
  local copies, waits for them, and re-layouts: 6.14 us -> 27.8 us
    ppermute x0 -> x15, waiting for transfers between devices: none -> 92.3 us  [the longest x8 85.5 us: collect(): lax.ppermute(going_up, axis, [(d, (d + 1) % ways) for d in range(ways)])]
    all_gather x1, waiting for transfers between devices: 74.9 us -> 0.01 us  [body(): rows_x = lax.all_gather(activations, 'expert', axis=0, tiled=True)]
    all_gather x1 -> x0, waiting for transfers between devices: 58 us -> none  [body(): rows_g = lax.all_gather(out_grad, 'expert', axis=0, tiled=True)]
    ppermute x0 -> x15, starting transfers between devices: none -> 40.3 us  [the longest x7 38.6 us: collect(): lax.ppermute(going_down, axis, [(d, (d - 1) % ways) for d in range(ways)])]
    dynamic_update_slice x0 -> x16, local copies, waits for them, and re-layouts: none -> 18.8 us  [the longest x7 9.09 us: collect(): lax.dynamic_update_slice_in_dim(full, going_down, (here + far) % ways * s...]
    unnamed x7 -> x6, waiting for transfers between devices: 74.7 us -> 71.5 us
  transfers between devices with their start and end apart: 6 -> 20, of which waited for: 5 -> 16; matrix products, arithmetic and copies ran while one was open for 12% -> 13% of each run, Pallas kernels for 0% -> 0%
where the time goes in v1:
time: 464 us
  waiting for transfers between devices  286 us (62%)
  matrix products  63.3 us (14%)
  starting transfers between devices  40.8 us (9%)
  local copies, waits for them, and re-layouts  27.8 us (6%)
  blocking collectives  23 us (5%)
  between operations  13.9 us (3%)
  other arithmetic  9.42 us (2%)
    reduce_scatter x1, waiting for transfers between devices, body(): lax.psum_scatter(slot_grad, 'expert', scatter_dimension=0, tiled=True)  86.5 us
    ppermute x8, waiting for transfers between devices, collect(): lax.ppermute(going_up, axis, [(d, (d + 1) % ways) for d in range(ways)])  85.5 us
    unnamed x6, waiting for transfers between devices  71.5 us
    ppermute x7, starting transfers between devices, collect(): lax.ppermute(going_down, axis, [(d, (d - 1) % ways) for d in range(ways)])  38.6 us
    reduce_scatter x1, waiting for transfers between devices, body(): lax.psum_scatter(lax.dot_general(rows_x, pre_grad, (((0,), (0,)), ((), ()...  35.3 us
    all_gather x1, blocking collectives, body(): tables = lax.all_gather(table, 'expert', axis=0, tiled=True)  23 us
    dot_general x1, matrix products, body(): pre = jnp.dot(rows_x, weight_gu, preferred_element_type=jnp.float32)  14.5 us
    dot_general x1, matrix products, body(): lax.dot_general(pre_grad, weight_gu, (((1,), (1,)), ((), ())), preferred_...  14.2 us
  transfers between devices with their start and end apart: 20, of which 16 were waited for; matrix products, arithmetic and copies ran while one was open for 13% of the time, Pallas kernels for 0%

profile of v1, /device:TPU:0, one launch (start us, length us, event | category | flops | bytes accessed | tf_op | source)
XLA Modules:
  0.0 463.8 jit_solution(9645489228323069640)
XLA Ops:
  8.0 1.7 collective-permute-start
  9.6 4.8 %collective-permute-start.1 = (bf16[128,2048]{1,0:T(8,128)(2,1)}, bf16[128,2048]{1,0:T(8,128)(2,1)}, u32[]{:S(2)}, u32[]{:S(2)}) collective-permute-start(bf16[128,2048]{1,0:T(8,128)(2,1)} %param.7), channel_id=1, source_target_pairs={{0,120},{8,0},{16,8},{24,16},{32,24},{40,32},{48,40},{56,48},{64,5... | collective-permute-start | bytes 1572872 | tf_op jit(solution)/shard_map/ppermute | solution.py:18
  14.5 12.1 %collective-permute-done = bf16[128,2048]{1,0:T(8,128)(2,1)S(1)} collective-permute-done((bf16[128,2048]{1,0:T(8,128)(2,1)}, bf16[128,2048]{1,0:T(8,128)(2,1)S(1)}, u32[]{:S(2)}, u32[]{:S(2)}) %collective-permute-start) | collective-permute-done | bytes 524320 | tf_op jit(solution)/shard_map/ppermute | solution.py:15
  26.5 2.7 collective-permute-done.1
  29.2 5.8 %collective-permute-start.3 = (bf16[128,2048]{1,0:T(8,128)(2,1)}, bf16[128,2048]{1,0:T(8,128)(2,1)}, u32[]{:S(2)}, u32[]{:S(2)}) collective-permute-start(bf16[128,2048]{1,0:T(8,128)(2,1)} %collective-permute-done.1), channel_id=1, source_target_pairs={{0,120},{8,0},{16,8},{24,16},{32,24},{40,32},{48,40},{56,48},{64,5... | collective-permute-start | bytes 1572872 | tf_op jit(solution)/shard_map/ppermute | solution.py:18
  35.0 13.8 %collective-permute-done.2 = bf16[128,2048]{1,0:T(8,128)(2,1)} collective-permute-done((bf16[128,2048]{1,0:T(8,128)(2,1)S(1)}, bf16[128,2048]{1,0:T(8,128)(2,1)}, u32[]{:S(2)}, u32[]{:S(2)}) %collective-permute-start.2) | collective-permute-done | bytes 524320 | tf_op jit(solution)/shard_map/ppermute | solution.py:15
  48.8 5.3 %collective-permute-start.5 = (bf16[128,2048]{1,0:T(8,128)(2,1)}, bf16[128,2048]{1,0:T(8,128)(2,1)}, u32[]{:S(2)}, u32[]{:S(2)}) collective-permute-start(bf16[128,2048]{1,0:T(8,128)(2,1)} %collective-permute-done.3), channel_id=1, source_target_pairs={{0,120},{8,0},{16,8},{24,16},{32,24},{40,32},{48,40},{56,48},{64,5... | collective-permute-start | bytes 1572872 | tf_op jit(solution)/shard_map/ppermute | solution.py:18
  54.1 4.6 broadcast_in_dim.45
  59.5 11.3 %collective-permute-done.4 = bf16[128,2048]{1,0:T(8,128)(2,1)S(1)} collective-permute-done((bf16[128,2048]{1,0:T(8,128)(2,1)}, bf16[128,2048]{1,0:T(8,128)(2,1)S(1)}, u32[]{:S(2)}, u32[]{:S(2)}) %collective-permute-start.4) | collective-permute-done | bytes 524320 | tf_op jit(solution)/shard_map/ppermute | solution.py:15
  70.8 1.9 constant_dynamic-update-slice_fusion.14
  72.8 2.7 collective-permute-done.5
  75.4 5.8 %collective-permute-start.7 = (bf16[128,2048]{1,0:T(8,128)(2,1)}, bf16[128,2048]{1,0:T(8,128)(2,1)S(1)}, u32[]{:S(2)}, u32[]{:S(2)}) collective-permute-start(bf16[128,2048]{1,0:T(8,128)(2,1)} %collective-permute-done.5), channel_id=1, source_target_pairs={{0,120},{8,0},{16,8},{24,16},{32,24},{40,32},{48,40},{56,48},{64,5... | collective-permute-start | bytes 1572872 | tf_op jit(solution)/shard_map/ppermute | solution.py:18
  81.2 1.9 constant_dynamic-update-slice_fusion.13
  83.1 15.1 %collective-permute-done.6 = bf16[128,2048]{1,0:T(8,128)(2,1)S(1)} collective-permute-done((bf16[128,2048]{1,0:T(8,128)(2,1)S(1)}, bf16[128,2048]{1,0:T(8,128)(2,1)S(1)}, u32[]{:S(2)}, u32[]{:S(2)}) %collective-permute-start.6) | collective-permute-done | bytes 524320 | tf_op jit(solution)/shard_map/ppermute | solution.py:15
  98.3 1.9 constant_dynamic-update-slice_fusion.12
  100.2 1.9 constant_dynamic-update-slice_fusion.11
  102.1 1.0 collective-permute-done.7
  103.1 5.7 %collective-permute-start.9 = (bf16[128,2048]{1,0:T(8,128)(2,1)S(1)}, bf16[128,2048]{1,0:T(8,128)(2,1)S(1)}, u32[]{:S(2)}, u32[]{:S(2)}) collective-permute-start(bf16[128,2048]{1,0:T(8,128)(2,1)S(1)} %collective-permute-done.7), channel_id=1, source_target_pairs={{0,120},{8,0},{16,8},{24,16},{32,24},{40,32},{48,40},{56,48},{64,5... | collective-permute-start | bytes 1572872 | tf_op jit(solution)/shard_map/ppermute | solution.py:18
  109.6 12.0 %collective-permute-done.8 = bf16[128,2048]{1,0:T(8,128)(2,1)S(1)} collective-permute-done((bf16[128,2048]{1,0:T(8,128)(2,1)S(1)}, bf16[128,2048]{1,0:T(8,128)(2,1)S(1)}, u32[]{:S(2)}, u32[]{:S(2)}) %collective-permute-start.8) | collective-permute-done | bytes 524320 | tf_op jit(solution)/shard_map/ppermute | solution.py:15
  121.6 1.9 constant_dynamic-update-slice_fusion.9
  123.5 0.8 constant_dynamic-update-slice_fusion.8
  124.4 5.4 %collective-permute-start.11 = (bf16[128,2048]{1,0:T(8,128)(2,1)S(1)}, bf16[128,2048]{1,0:T(8,128)(2,1)S(1)}, u32[]{:S(2)}, u32[]{:S(2)}) collective-permute-start(bf16[128,2048]{1,0:T(8,128)(2,1)S(1)} %collective-permute-done.9), channel_id=1, source_target_pairs={{0,120},{8,0},{16,8},{24,16},{32,24},{40,32},{48,40},{56,48},{64,5... | collective-permute-start | bytes 1572872 | tf_op jit(solution)/shard_map/ppermute | solution.py:18
  129.7 0.9 constant_dynamic-update-slice_fusion.7
  130.6 5.7 %collective-permute-done.10 = bf16[128,2048]{1,0:T(8,128)(2,1)S(1)} collective-permute-done((bf16[128,2048]{1,0:T(8,128)(2,1)S(1)}, bf16[128,2048]{1,0:T(8,128)(2,1)S(1)}, u32[]{:S(2)}, u32[]{:S(2)}) %collective-permute-start.10) | collective-permute-done | bytes 524320 | tf_op jit(solution)/shard_map/ppermute | solution.py:15
  136.3 0.8 constant_dynamic-update-slice_fusion.6
  137.2 0.8 constant_dynamic-update-slice_fusion.5
  138.3 5.8 %collective-permute-start.13 = (bf16[128,2048]{1,0:T(8,128)(2,1)S(1)}, bf16[128,2048]{1,0:T(8,128)(2,1)S(1)}, u32[]{:S(2)}, u32[]{:S(2)}) collective-permute-start(bf16[128,2048]{1,0:T(8,128)(2,1)S(1)} %collective-permute-done.11), channel_id=1, source_target_pairs={{0,120},{8,0},{16,8},{24,16},{32,24},{40,32},{48,40},{56,48},{64,5... | collective-permute-start | bytes 1572872 | tf_op jit(solution)/shard_map/ppermute | solution.py:18
  144.1 0.9 constant_dynamic-update-slice_fusion.4
  145.0 5.1 %collective-permute-done.12 = bf16[128,2048]{1,0:T(8,128)(2,1)S(1)} collective-permute-done((bf16[128,2048]{1,0:T(8,128)(2,1)S(1)}, bf16[128,2048]{1,0:T(8,128)(2,1)S(1)}, u32[]{:S(2)}, u32[]{:S(2)}) %collective-permute-start.12) | collective-permute-done | bytes 524320 | tf_op jit(solution)/shard_map/ppermute | solution.py:15
  150.1 0.8 constant_dynamic-update-slice_fusion.3
  151.0 0.8 constant_dynamic-update-slice_fusion.2
  151.9 0.8 constant_dynamic-update-slice_fusion.1
  152.7 10.4 %collective-permute-done.14 = bf16[128,2048]{1,0:T(8,128)(2,1)S(1)} collective-permute-done((bf16[128,2048]{1,0:T(8,128)(2,1)S(1)}, bf16[128,2048]{1,0:T(8,128)(2,1)S(1)}, u32[]{:S(2)}, u32[]{:S(2)}) %collective-permute-start.14) | collective-permute-done | bytes 524320 | tf_op jit(solution)/shard_map/ppermute | solution.py:15
  163.9 14.5 %fusion.3 = f32[2048,1024]{0,1:T(8,128)} fusion(bf16[2048,2048]{1,0:T(8,128)(2,1)} %all-gather.2.cloned.1.call-done, bf16[1,2048,1024]{2,1,0:T(8,128)(2,1)} %param.10), kind=kOutput, calls=%fused_computation.7 | convolution fusion | flops 8589934592 | bytes 20971520 | tf_op jit(solution)/shard_map/dot_general | solution.py:41
  178.5 11.9 %fusion = (f32[2048]{0:T(1024)S(1)}, bf16[2048,512]{0,1:T(8,128)(2,1)}, f32[2048,512]{0,1:T(8,128)}) fusion(f32[2048,1024]{0,1:T(8,128)} %fusion.3, bf16[2048,2048]{1,0:T(8,128)(2,1)} %constant_dynamic-update-slice_fusion, bf16[1,2048,512]{2,1,0:T(8,128)(2,1)S(1)} %copy-done), kind=kOutput, calls=%fused_computation.3 | convolution fusion | flops 4304402432 | bytes 25174016 | tf_op jit(solution)/shard_map/dot_general | solution.py:46
  190.4 1.0 copy.15
  191.5 70.8 %reduce-scatter.13.cloned.1.call-done = bf16[128,16]{1,0:T(8,128)(2,1)} async-done(((bf16[2048,16]{1,0:T(8,128)(2,1)}), bf16[128,16]{1,0:T(8,128)(2,1)}) %reduce-scatter.13.cloned.1.call-update) | async-done | bytes 4112
  263.7 23.0 %all_gather.6 = bf16[2048,16]{0,1:T(8,128)(2,1)S(1)} all-gather(bf16[128,16]{0,1:T(8,128)(2,1)S(1)} %get-tuple-element.17), channel_id=1, replica_groups=mesh['expert'=16,'group'=8] {'expert'}, dimensions={0}, use_global_device_ids=true | all-gather | bytes 69632 | tf_op jit(solution)/shard_map/all_gather | solution.py:35
  286.8 9.9 %convolution_convert_fusion.1 = bf16[2048,512]{1,0:T(8,128)(2,1)} fusion(bf16[2048,2048]{1,0:T(8,128)(2,1)} %constant_dynamic-update-slice_fusion, bf16[2048,512]{0,1:T(8,128)(2,1)} %get-tuple-element.19, f32[2048]{0:T(1024)S(1)} %multiply_reduce_fusion), kind=kOutput, calls=%fused_computation.14 | convolution fusion | flops 4299161600 | bytes 12591104 | tf_op jit(solution)/shard_map/dot_general | solution.py:72
  296.8 5.7 %multiply_convert_fusion.2 = (bf16[2048,512]{0,1:T(8,128)(2,1)S(1)}, bf16[2048,512]{0,1:T(8,128)(2,1)S(1)}) fusion(f32[2048,1024]{0,1:T(8,128)} %fusion.3, f32[2048,512]{0,1:T(8,128)} %get-tuple-element.22, f32[2048]{0:T(1024)S(1)} %multiply_reduce_fusion), kind=kLoop, calls=%fused_computation.12 | loop fusion | flops 14680064 | bytes 16785408 | tf_op jit(solution)/shard_map/convert.2
  302.6 1.3 copy-done.3
  303.9 12.8 %convert_bitcast_fusion = bf16[2048,1024]{0,1:T(8,128)(2,1)} fusion(bf16[2048,2048]{1,0:T(8,128)(2,1)} %all-gather.2.cloned.1.call-done, bf16[2048,512]{0,1:T(8,128)(2,1)S(1)} %get-tuple-element.21, bf16[2048,512]{0,1:T(8,128)(2,1)S(1)} %get-tuple-element.20), kind=kOutput, calls=%fused_computation.9 | convolution fusion | flops 8600420352 | bytes 16777216 | tf_op jit(solution)/shard_map/dot_general | solution.py:64
  317.1 14.2 %convolution_convert_fusion = bf16[2048,2048]{1,0:T(8,128)(2,1)} fusion(bf16[1,2048,1024]{2,1,0:T(8,128)(2,1)} %param.10, bf16[2048,512]{0,1:T(8,128)(2,1)} %copy-done.3, bf16[2048,512]{0,1:T(8,128)(2,1)} %copy-done.2), kind=kOutput, calls=%fused_computation | convolution fusion | flops 8602517504 | bytes 16777216 | tf_op jit(solution)/shard_map/dot_general | solution.py:53
  331.3 1.8 bitcast_convert_fusion.1
  333.1 35.3 %reduce-scatter.9.cloned.1.call-done = bf16[256,1024]{0,1:T(8,128)(2,1)} async-done(((bf16[2048,1024]{0,1:T(8,128)(2,1)}), bf16[256,1024]{0,1:T(8,128)(2,1)}) %reduce-scatter.9.cloned.1.call-update) | async-done | bytes 524304 | tf_op jit(solution)/shard_map/reduce_scatter | solution.py:63
  368.4 1.1 bitcast_convert_fusion
  369.5 1.3 copy.14
  370.8 86.5 %reduce-scatter.7.cloned.1.call-done = bf16[128,2048]{1,0:T(8,128)(2,1)} async-done(((bf16[2048,2048]{1,0:T(8,128)(2,1)}), bf16[128,2048]{1,0:T(8,128)(2,1)}) %reduce-scatter.7.cloned.1.call-update) | async-done | bytes 524304 | tf_op jit(solution)/shard_map/reduce_scatter | solution.py:56
  (48 shorter events, 5.8 us)
Async XLA Ops:
  7.2 171.3 %copy-start = (bf16[1,2048,512]{2,1,0:T(8,128)(2,1)S(1)}, bf16[1,2048,512]{2,1,0:T(8,128)(2,1)}, u32[]{:S(2)}) copy-start(bf16[1,2048,512]{2,1,0:T(8,128)(2,1)} %param.11) | copy-start | bytes 6291460
  7.2 51.5 %copy-start.4 = (bf16[128,2048]{1,0:T(8,128)(2,1)S(1)}, bf16[128,2048]{1,0:T(8,128)(2,1)}, u32[]{:S(2)}) copy-start(bf16[128,2048]{1,0:T(8,128)(2,1)} %param.7) | copy-start | bytes 1572868
  7.2 156.7 %all-gather.2.cloned.1.call-start = ((), (), s32[]{:S(2)}) async-start(), calls=%async_computation.4 | async-start | bytes 8912896 | tf_op jit(solution)/shard_map/all_gather | solution.py:33
  7.9 254.4 %reduce-scatter.13.cloned.1.call-start = ((), (), s32[]{:S(2)}) async-start(), calls=%async_computation.8 | async-start | bytes 557056
  8.0 18.5 %collective-permute-start = (bf16[128,2048]{1,0:T(8,128)(2,1)}, bf16[128,2048]{1,0:T(8,128)(2,1)S(1)}, u32[]{:S(2)}, u32[]{:S(2)}) collective-permute-start(bf16[128,2048]{1,0:T(8,128)(2,1)} %param.7), channel_id=1, source_target_pairs={{0,8},{8,16},{16,24},{24,32},{32,40},{40,48},{48,56},{56,64},{64,7... | collective-permute-start | bytes 1572872 | tf_op jit(solution)/shard_map/ppermute | solution.py:15
  9.6 19.5 %collective-permute-start.1 = (bf16[128,2048]{1,0:T(8,128)(2,1)}, bf16[128,2048]{1,0:T(8,128)(2,1)}, u32[]{:S(2)}, u32[]{:S(2)}) collective-permute-start(bf16[128,2048]{1,0:T(8,128)(2,1)} %param.7), channel_id=1, source_target_pairs={{0,120},{8,0},{16,8},{24,16},{32,24},{40,32},{48,40},{56,48},{64,5... | collective-permute-start | bytes 1572872 | tf_op jit(solution)/shard_map/ppermute | solution.py:18
  26.5 8.5 %copy-start.5 = (bf16[128,2048]{1,0:T(8,128)(2,1)}, bf16[128,2048]{1,0:T(8,128)(2,1)S(1)}, u32[]{:S(2)}) copy-start(bf16[128,2048]{1,0:T(8,128)(2,1)S(1)} %collective-permute-done) | copy-start | bytes 1572868
  26.5 22.3 %collective-permute-start.2 = (bf16[128,2048]{1,0:T(8,128)(2,1)S(1)}, bf16[128,2048]{1,0:T(8,128)(2,1)}, u32[]{:S(2)}, u32[]{:S(2)}) collective-permute-start(bf16[128,2048]{1,0:T(8,128)(2,1)S(1)} %collective-permute-done), channel_id=1, source_target_pairs={{0,8},{8,16},{16,24},{24,32},{32,40},{40,48},{48,56},{56,64},{64,7... | collective-permute-start | bytes 1572872 | tf_op jit(solution)/shard_map/ppermute | solution.py:15
  29.2 19.6 %collective-permute-start.3 = (bf16[128,2048]{1,0:T(8,128)(2,1)}, bf16[128,2048]{1,0:T(8,128)(2,1)}, u32[]{:S(2)}, u32[]{:S(2)}) collective-permute-start(bf16[128,2048]{1,0:T(8,128)(2,1)} %collective-permute-done.1), channel_id=1, source_target_pairs={{0,120},{8,0},{16,8},{24,16},{32,24},{40,32},{48,40},{56,48},{64,5... | collective-permute-start | bytes 1572872 | tf_op jit(solution)/shard_map/ppermute | solution.py:18
  48.8 22.0 %collective-permute-start.4 = (bf16[128,2048]{1,0:T(8,128)(2,1)}, bf16[128,2048]{1,0:T(8,128)(2,1)S(1)}, u32[]{:S(2)}, u32[]{:S(2)}) collective-permute-start(bf16[128,2048]{1,0:T(8,128)(2,1)} %collective-permute-done.2), channel_id=1, source_target_pairs={{0,8},{8,16},{16,24},{24,32},{32,40},{40,48},{48,56},{56,64},{64,7... | collective-permute-start | bytes 1572872 | tf_op jit(solution)/shard_map/ppermute | solution.py:15
  48.8 26.6 %collective-permute-start.5 = (bf16[128,2048]{1,0:T(8,128)(2,1)}, bf16[128,2048]{1,0:T(8,128)(2,1)}, u32[]{:S(2)}, u32[]{:S(2)}) collective-permute-start(bf16[128,2048]{1,0:T(8,128)(2,1)} %collective-permute-done.3), channel_id=1, source_target_pairs={{0,120},{8,0},{16,8},{24,16},{32,24},{40,32},{48,40},{56,48},{64,5... | collective-permute-start | bytes 1572872 | tf_op jit(solution)/shard_map/ppermute | solution.py:18
  70.8 27.4 %collective-permute-start.6 = (bf16[128,2048]{1,0:T(8,128)(2,1)S(1)}, bf16[128,2048]{1,0:T(8,128)(2,1)S(1)}, u32[]{:S(2)}, u32[]{:S(2)}) collective-permute-start(bf16[128,2048]{1,0:T(8,128)(2,1)S(1)} %collective-permute-done.4), channel_id=1, source_target_pairs={{0,8},{8,16},{16,24},{24,32},{32,40},{40,48},{48,56},{56,64},{64,7... | collective-permute-start | bytes 1572872 | tf_op jit(solution)/shard_map/ppermute | solution.py:15
  75.4 27.7 %collective-permute-start.7 = (bf16[128,2048]{1,0:T(8,128)(2,1)}, bf16[128,2048]{1,0:T(8,128)(2,1)S(1)}, u32[]{:S(2)}, u32[]{:S(2)}) collective-permute-start(bf16[128,2048]{1,0:T(8,128)(2,1)} %collective-permute-done.5), channel_id=1, source_target_pairs={{0,120},{8,0},{16,8},{24,16},{32,24},{40,32},{48,40},{56,48},{64,5... | collective-permute-start | bytes 1572872 | tf_op jit(solution)/shard_map/ppermute | solution.py:18
  98.3 23.4 %collective-permute-start.8 = (bf16[128,2048]{1,0:T(8,128)(2,1)S(1)}, bf16[128,2048]{1,0:T(8,128)(2,1)S(1)}, u32[]{:S(2)}, u32[]{:S(2)}) collective-permute-start(bf16[128,2048]{1,0:T(8,128)(2,1)S(1)} %collective-permute-done.6), channel_id=1, source_target_pairs={{0,8},{8,16},{16,24},{24,32},{32,40},{40,48},{48,56},{56,64},{64,7... | collective-permute-start | bytes 1572872 | tf_op jit(solution)/shard_map/ppermute | solution.py:15
  103.1 21.3 %collective-permute-start.9 = (bf16[128,2048]{1,0:T(8,128)(2,1)S(1)}, bf16[128,2048]{1,0:T(8,128)(2,1)S(1)}, u32[]{:S(2)}, u32[]{:S(2)}) collective-permute-start(bf16[128,2048]{1,0:T(8,128)(2,1)S(1)} %collective-permute-done.7), channel_id=1, source_target_pairs={{0,120},{8,0},{16,8},{24,16},{32,24},{40,32},{48,40},{56,48},{64,5... | collective-permute-start | bytes 1572872 | tf_op jit(solution)/shard_map/ppermute | solution.py:18
  121.6 14.7 %collective-permute-start.10 = (bf16[128,2048]{1,0:T(8,128)(2,1)S(1)}, bf16[128,2048]{1,0:T(8,128)(2,1)S(1)}, u32[]{:S(2)}, u32[]{:S(2)}) collective-permute-start(bf16[128,2048]{1,0:T(8,128)(2,1)S(1)} %collective-permute-done.8), channel_id=1, source_target_pairs={{0,8},{8,16},{16,24},{24,32},{32,40},{40,48},{48,56},{56,64},{64,7... | collective-permute-start | bytes 1572872 | tf_op jit(solution)/shard_map/ppermute | solution.py:15
  124.4 14.0 %collective-permute-start.11 = (bf16[128,2048]{1,0:T(8,128)(2,1)S(1)}, bf16[128,2048]{1,0:T(8,128)(2,1)S(1)}, u32[]{:S(2)}, u32[]{:S(2)}) collective-permute-start(bf16[128,2048]{1,0:T(8,128)(2,1)S(1)} %collective-permute-done.9), channel_id=1, source_target_pairs={{0,120},{8,0},{16,8},{24,16},{32,24},{40,32},{48,40},{56,48},{64,5... | collective-permute-start | bytes 1572872 | tf_op jit(solution)/shard_map/ppermute | solution.py:18
  136.3 13.8 %collective-permute-start.12 = (bf16[128,2048]{1,0:T(8,128)(2,1)S(1)}, bf16[128,2048]{1,0:T(8,128)(2,1)S(1)}, u32[]{:S(2)}, u32[]{:S(2)}) collective-permute-start(bf16[128,2048]{1,0:T(8,128)(2,1)S(1)} %collective-permute-done.10), channel_id=1, source_target_pairs={{0,8},{8,16},{16,24},{24,32},{32,40},{40,48},{48,56},{56,64},{64,7... | collective-permute-start | bytes 1572872 | tf_op jit(solution)/shard_map/ppermute | solution.py:15
  138.3 13.5 %collective-permute-start.13 = (bf16[128,2048]{1,0:T(8,128)(2,1)S(1)}, bf16[128,2048]{1,0:T(8,128)(2,1)S(1)}, u32[]{:S(2)}, u32[]{:S(2)}) collective-permute-start(bf16[128,2048]{1,0:T(8,128)(2,1)S(1)} %collective-permute-done.11), channel_id=1, source_target_pairs={{0,120},{8,0},{16,8},{24,16},{32,24},{40,32},{48,40},{56,48},{64,5... | collective-permute-start | bytes 1572872 | tf_op jit(solution)/shard_map/ppermute | solution.py:18
  150.1 13.0 %collective-permute-start.14 = (bf16[128,2048]{1,0:T(8,128)(2,1)S(1)}, bf16[128,2048]{1,0:T(8,128)(2,1)S(1)}, u32[]{:S(2)}, u32[]{:S(2)}) collective-permute-start(bf16[128,2048]{1,0:T(8,128)(2,1)S(1)} %collective-permute-done.12), channel_id=1, source_target_pairs={{0,8},{8,16},{16,24},{24,32},{32,40},{40,48},{48,56},{56,64},{64,7... | collective-permute-start | bytes 1572872 | tf_op jit(solution)/shard_map/ppermute | solution.py:15
  178.5 13.1 %copy-start.7 = (bf16[128,4]{0,1:T(4,128)(2,1)S(1)}, bf16[128,4]{0,1:T(4,128)(2,1)}, u32[]{:S(2)}) copy-start(bf16[128,4]{0,1:T(4,128)(2,1)} %param.8) | copy-start | bytes 3076
  178.5 84.6 %copy-start.6 = (s32[128,4]{0,1:T(4,128)S(1)}, s32[128,4]{0,1:T(4,128)}, u32[]{:S(2)}) copy-start(s32[128,4]{0,1:T(4,128)} %param.9) | copy-start | bytes 6148
  191.5 139.8 %reduce-scatter.11.cloned.1.call-start = ((), (), s32[]{:S(2)}) async-start(), calls=%async_computation.7 | async-start | bytes 2359296 | tf_op jit(solution)/shard_map/reduce_scatter | solution.py:71
  296.8 71.6 %reduce-scatter.9.cloned.1.call-start = ((), (), s32[]{:S(2)}) async-start(), calls=%async_computation.6 | async-start | bytes 4718592 | tf_op jit(solution)/shard_map/reduce_scatter | solution.py:63
  302.5 1.3 copy-start.3
  302.6 14.2 %copy-start.2 = (bf16[2048,512]{0,1:T(8,128)(2,1)}, bf16[2048,512]{0,1:T(8,128)(2,1)S(1)}, u32[]{:S(2)}) copy-start(bf16[2048,512]{0,1:T(8,128)(2,1)S(1)} %get-tuple-element.20) | copy-start | bytes 6291460
  316.7 140.6 %reduce-scatter.7.cloned.1.call-start = ((), (), s32[]{:S(2)}) async-start(), calls=%async_computation.5 | async-start | bytes 8912896 | tf_op jit(solution)/shard_map/reduce_scatter | solution.py:56
  317.1 140.2 %copy-start.1 = (bf16[1,2048,512]{2,1,0:T(8,128)(2,1)S(1)}, bf16[1,2048,512]{2,1,0:T(8,128)(2,1)}, u32[]{:S(2)}) copy-start(bf16[1,2048,512]{2,1,0:T(8,128)(2,1)} %param.11) | copy-start | bytes 6291460
Sparse Core Ops, SparseCore 0:
  10.1 110.0 all-gather.1
  191.6 70.6 reduce-scatter.12
  296.9 32.5 reduce-scatter.10
  331.7 36.6 reduce-scatter.8
  372.2 85.0 reduce-scatter.6
